TPU v7x, 32 devices: a whole 2x2x4 slice. The times are simulated.
32 devices in a mesh: row: 8 (over y, x, core), col: 4 (over z).
Axes of the slice: x: 2, y: 2, z: 4, core: 2. Of those that a mesh axis runs over, the one named last changes fastest.
Arguments:
- documents: float32 [6144, 768], P('row', 'col'), may hold values from -6 to 6
- projection: float32 [768, 768], P('col'), may hold values from -0.21875 to 0.21875
- landmarks: float32 [16384, 768], P('col', 'row'), may hold values from -6 to 6
- coefficients: float32 [16384, 128], P('col'), may hold values from -6 to 6
- inverse_tiles: float32 [16384, 16384], P('col', 'row'), may hold values from -0.046875 to 0.046875
- labels: int32 [6144, 128], P('row'), may hold values 0 or 1
Outputs:
- new_coefficients: float32 [16384, 128], P('col')
- residual: float32 [6144, 128], P('row')
All inputs are finite; a program needn't handle non-finite values. No bound on the sum of `labels` on one device may be relied on, other than what follows from the above.
Results may differ from a plain program's by a relative error of at most 0.0001.
Values sent between devices are 32-bit elements; how exact they have to be, the bound alone decides.
A program may use at most 128 MiB of HBM per device.

v0:
```python
import jax
import jax.numpy as jnp
from jax import lax
from jax.sharding import PartitionSpec as P

ITERS = 2


def broadcast(block, axis, owner):
    block = jnp.where(lax.axis_index(axis) == owner, block, jnp.zeros_like(block))
    return lax.psum(block, axis)


def on_device(documents, projection, landmarks, coefficients, inverse_tiles, labels):
    highest = lax.Precision.HIGHEST
    land_full = lax.all_gather(landmarks, "row", axis=1, tiled=True)
    sq_land = jnp.sum(land_full * land_full, axis=1)
    feature_width = land_full.shape[1]
    proj_share = lax.psum_scatter(
        jnp.dot(documents, projection, precision=highest, preferred_element_type=jnp.float32),
        "col",
        scatter_dimension=0,
        tiled=True,
    )
    rows_in = lax.all_gather(proj_share, "col", axis=0, tiled=True)
    sq_doc = jnp.sum(rows_in * rows_in, axis=1)
    inner = lax.dot_general(
        rows_in,
        land_full,
        (((1,), (1,)), ((), ())),
        precision=highest,
        preferred_element_type=jnp.float32,
    )
    kernel = jnp.exp(-2.0 * (sq_doc[:, None] + sq_land[None, :] - 2.0 * inner) / feature_width)
    row_count = lax.axis_size("row")
    col_count = lax.axis_size("col")
    step_size = 64.0 / (documents.shape[0] * row_count)
    block_rows = inverse_tiles.shape[1]
    group_size = row_count // col_count
    row_index = lax.axis_index("row")
    source = row_index // group_size
    offset = row_index % group_size * block_rows
    current = coefficients
    target = labels.astype(jnp.float32)
    residual = jnp.zeros((documents.shape[0], labels.shape[1]), jnp.float32)
    for iteration in range(ITERS):
        local_pred = jnp.dot(kernel, current, precision=highest, preferred_element_type=jnp.float32)
        predicted = lax.psum(local_pred, "col")
        residual = jax.nn.sigmoid(predicted) - target
        local_grad = lax.dot_general(
            kernel,
            residual,
            (((0,), (0,)), ((), ())),
            precision=highest,
            preferred_element_type=jnp.float32,
        )
        gradient = lax.psum(local_grad, "row")
        grad_block = lax.dynamic_slice_in_dim(gradient, offset, block_rows, 0)
        grad_block = broadcast(grad_block, "col", source)
        product_term = jnp.dot(
            inverse_tiles, grad_block, precision=highest, preferred_element_type=jnp.float32
        )
        current = current - step_size * lax.psum(product_term, "row")
    return (current, residual)


def solution(mesh):
    in_specs = (
        P("row", "col"),
        P("col", None),
        P("col", "row"),
        P("col", None),
        P("col", "row"),
        P("row", None),
    )
    out_specs = (P("col", None), P("row", None))
    return jax.shard_map(
        on_device, mesh=mesh, in_specs=in_specs, out_specs=out_specs, check_vma=False
    )
```

profile of v0, /device:TPU:0, one launch (start us, length us, event | category | flops | bytes accessed | tf_op | source)
XLA Modules:
  0.0 830.2 jit_solution(13493316278043722178)
XLA Ops:
  8.2 4.6 fusion.11
  12.9 50.5 %reduce-scatter.2.cloned.1.call-done = f32[192,768]{1,0:T(8,128)} async-done(((f32[768,768]{1,0:T(8,128)}), f32[192,768]{1,0:T(8,128)}) %reduce-scatter.2.cloned.1.call-update) | async-done | bytes 589840 | tf_op jit(solution)/shard_map/reduce_scatter | solution.py:19
  64.2 50.2 %all-gather.3.cloned.1.call-done = f32[768,768]{1,0:T(8,128)} async-done(((f32[192,768]{1,0:T(8,128)}), f32[768,768]{1,0:T(8,128)}) %all-gather.3.cloned.1.call-update) | async-done | bytes 2359312 | tf_op jit(solution)/shard_map/all_gather | solution.py:25
  116.4 70.6 %all-gather.5.cloned.1.call-done = f32[4096,768]{0,1:T(8,128)} async-done(((f32[4096,96]{0,1:T(8,128)}), f32[4096,768]{0,1:T(8,128)}) %all-gather.5.cloned.1.call-update) | async-done | bytes 12582928 | tf_op jit(solution)/shard_map/all_gather | solution.py:16
  187.1 5.9 multiply_reduce_fusion
  192.9 2.3 copy-done.3
  195.2 32.1 %multiply_exponential_fusion = f32[768,4096]{1,0:T(8,128)S(1)} fusion(f32[768,768]{1,0:T(8,128)S(1)} %copy-done.5, f32[4096,768]{0,1:T(8,128)S(1)} %copy-done.3, f32[4096]{0:T(1024)S(1)} %multiply_reduce_fusion, f32[768]{0:T(1024)S(1)} %multiply_reduce_fusion.1), kind=kOutput, calls=%fused_computation | convolution fusion | flops 29003612160 | bytes 27544576 | tf_op jit(solution)/shard_map/dot_general | solution.py:27
  227.4 4.5 copy-done.2
  231.9 10.6 %fusion.12 = f32[768,128]{1,0:T(8,128)} fusion(f32[768,4096]{1,0:T(8,128)S(1)} %multiply_exponential_fusion, f32[4096,128]{1,0:T(8,128)S(1)} %copy-done.4), kind=kOutput, calls=%fused_computation.22 | convolution fusion | flops 4831838208 | bytes 15073280 | tf_op jit(solution)/shard_map/dot_general | solution.py:47
  242.6 37.0 %all-reduce.9.cloned.1.call-done = f32[768,128]{1,0:T(8,128)} async-done(((f32[768,128]{1,0:T(8,128)}), f32[768,128]{1,0:T(8,128)}) %all-reduce.9.cloned.1.call-update) | async-done | bytes 393232 | tf_op jit(solution)/shard_map/psum | solution.py:48
  279.7 24.0 %fusion.1 = f32[4096,128]{1,0:T(8,128)} fusion(f32[768,4096]{1,0:T(8,128)} %copy-done.2, s32[768,128]{1,0:T(8,128)S(1)} %copy-done.6, f32[768,128]{1,0:T(8,128)} %all-reduce.9.cloned.1.call-done), kind=kOutput, calls=%fused_computation.11 | convolution fusion | flops 4832329728 | bytes 15466496 | tf_op jit(solution)/shard_map/dot_general | solution.py:50
  303.8 61.6 %all-reduce.11.cloned.1.call-done = f32[4096,128]{1,0:T(8,128)} async-done(((f32[4096,128]{1,0:T(8,128)}), f32[4096,128]{1,0:T(8,128)}) %all-reduce.11.cloned.1.call-update) | async-done | bytes 2097168 | tf_op jit(solution)/shard_map/psum | solution.py:57
  367.7 51.5 %all-reduce.13.cloned.1.call-done = f32[2048,128]{1,0:T(8,128)} async-done(((f32[2048,128]{1,0:T(8,128)}), f32[2048,128]{1,0:T(8,128)}) %all-reduce.13.cloned.1.call-update) | async-done | bytes 1048592 | tf_op jit(solution)/shard_map/psum | solution.py:11
  419.1 42.4 %convolution_bitcast_fusion.1 = f32[4096,128]{0,1:T(8,128)} fusion(f32[2048,128]{1,0:T(8,128)} %all-reduce.13.cloned.1.call-done, f32[4096,2048]{1,0:T(8,128)} %param.10), kind=kOutput, calls=%fused_computation.3 | convolution fusion | flops 12884901888 | bytes 36700160 | tf_op jit(solution)/shard_map/dot_general | solution.py:60
  463.6 59.2 %all-reduce.15.cloned.1.call-done = f32[4096,128]{0,1:T(8,128)} async-done(((f32[4096,128]{0,1:T(8,128)}), f32[4096,128]{0,1:T(8,128)}) %all-reduce.15.cloned.1.call-update) | async-done | bytes 2097168 | tf_op jit(solution)/shard_map/psum | solution.py:63
  522.8 13.9 %fusion = f32[768,128]{1,0:T(8,128)} fusion(f32[768,4096]{1,0:T(8,128)} %copy-done.2, f32[4096,128]{0,1:T(8,128)S(1)} %copy.8, f32[4096,128]{0,1:T(8,128)} %all-reduce.15.cloned.1.call-done), kind=kOutput, calls=%fused_computation.9 | convolution fusion | flops 4832886784 | bytes 17170432 | tf_op jit(solution)/shard_map/dot_general | solution.py:47
  536.7 36.1 %all-reduce.17.cloned.1.call-done = f32[768,128]{1,0:T(8,128)} async-done(((f32[768,128]{1,0:T(8,128)}), f32[768,128]{1,0:T(8,128)}) %all-reduce.17.cloned.1.call-update) | async-done | bytes 393232 | tf_op jit(solution)/shard_map/psum | solution.py:48
  574.0 23.8 %fusion.13 = f32[4096,128]{1,0:T(8,128)} fusion(f32[768,4096]{1,0:T(8,128)} %copy-done.2, f32[768,128]{1,0:T(8,128)S(1)} %divide_subtract_fusion), kind=kOutput, calls=%fused_computation.23 | convolution fusion | flops 4831838208 | bytes 15073280 | tf_op jit(solution)/shard_map/dot_general | solution.py:50
  597.9 61.6 %all-reduce.19.cloned.1.call-done = f32[4096,128]{1,0:T(8,128)} async-done(((f32[4096,128]{1,0:T(8,128)}), f32[4096,128]{1,0:T(8,128)}) %all-reduce.19.cloned.1.call-update) | async-done | bytes 2097168 | tf_op jit(solution)/shard_map/psum | solution.py:57
  661.9 51.4 %all-reduce.21.cloned.1.call-done = f32[2048,128]{1,0:T(8,128)} async-done(((f32[2048,128]{1,0:T(8,128)}), f32[2048,128]{1,0:T(8,128)}) %all-reduce.21.cloned.1.call-update) | async-done | bytes 1048592 | tf_op jit(solution)/shard_map/psum | solution.py:11
  713.3 42.0 %convolution_bitcast_fusion = f32[4096,128]{0,1:T(8,128)} fusion(f32[2048,128]{1,0:T(8,128)} %all-reduce.21.cloned.1.call-done, f32[4096,2048]{1,0:T(8,128)} %param.10), kind=kOutput, calls=%fused_computation.2 | convolution fusion | flops 12884901888 | bytes 36700160 | tf_op jit(solution)/shard_map/dot_general | solution.py:60
  755.4 61.2 %all-reduce.23.cloned.1.call-done = f32[4096,128]{0,1:T(8,128)} async-done(((f32[4096,128]{0,1:T(8,128)}), f32[4096,128]{0,1:T(8,128)}) %all-reduce.23.cloned.1.call-update) | async-done | bytes 2097168 | tf_op jit(solution)/shard_map/psum | solution.py:63
  816.5 4.0 multiply_subtract_fusion
  820.6 2.9 copy.9
  (41 shorter events, 11.9 us)
Async XLA Ops:
  7.2 1.1 copy-start
  7.2 56.2 %reduce-scatter.2.cloned.1.call-start = ((), (), s32[]{:S(2)}) async-start(), calls=%async_computation.1 | async-start | bytes 2949120 | tf_op jit(solution)/shard_map/reduce_scatter | solution.py:19
  12.8 101.5 %all-gather.3.cloned.1.call-start = ((), (), s32[]{:S(2)}) async-start(), calls=%async_computation.2 | async-start | bytes 2949120 | tf_op jit(solution)/shard_map/all_gather | solution.py:25
  63.4 123.6 %all-gather.5.cloned.1.call-start = ((), (), s32[]{:S(2)}) async-start(), calls=%async_computation.3 | async-start | bytes 14155776 | tf_op jit(solution)/shard_map/all_gather | solution.py:16
  64.2 215.5 %all-reduce.9.cloned.1.call-start = ((), (), s32[]{:S(2)}) async-start(), calls=%async_computation.4 | async-start | bytes 786432 | tf_op jit(solution)/shard_map/psum | solution.py:48
  114.4 78.6 %copy-start.5 = (f32[768,768]{1,0:T(8,128)S(1)}, f32[768,768]{1,0:T(8,128)}, u32[]{:S(2)}) copy-start(f32[768,768]{1,0:T(8,128)} %all-gather.3.cloned.1.call-done) | copy-start | bytes 7077892
  187.1 8.2 copy-start.3
  195.2 36.7 %copy-start.4 = (f32[4096,128]{1,0:T(8,128)S(1)}, f32[4096,128]{1,0:T(8,128)}, u32[]{:S(2)}) copy-start(f32[4096,128]{1,0:T(8,128)} %param.9) | copy-start | bytes 6291460
  227.4 4.5 copy-start.2
  231.9 47.8 %copy-start.6 = (s32[768,128]{1,0:T(8,128)S(1)}, s32[768,128]{1,0:T(8,128)}, u32[]{:S(2)}) copy-start(s32[768,128]{1,0:T(8,128)} %param.11) | copy-start | bytes 1179652
  242.6 122.8 %all-reduce.11.cloned.1.call-start = ((), (), s32[]{:S(2)}) async-start(), calls=%async_computation.5 | async-start | bytes 4194304 | tf_op jit(solution)/shard_map/psum | solution.py:57
  303.7 115.4 %all-reduce.13.cloned.1.call-start = ((), (), s32[]{:S(2)}) async-start(), calls=%async_computation.6 | async-start | bytes 2097152 | tf_op jit(solution)/shard_map/psum | solution.py:11
  367.6 155.1 %all-reduce.15.cloned.1.call-start = ((), (), s32[]{:S(2)}) async-start(), calls=%async_computation.7 | async-start | bytes 4194304 | tf_op jit(solution)/shard_map/psum | solution.py:63
  461.6 111.3 %all-reduce.17.cloned.1.call-start = ((), (), s32[]{:S(2)}) async-start(), calls=%async_computation.8 | async-start | bytes 786432 | tf_op jit(solution)/shard_map/psum | solution.py:48
  536.7 122.8 %all-reduce.19.cloned.1.call-start = ((), (), s32[]{:S(2)}) async-start(), calls=%async_computation.9 | async-start | bytes 4194304 | tf_op jit(solution)/shard_map/psum | solution.py:57
  574.0 23.8 %copy-start.7 = (f32[768,128]{1,0:T(8,128)}, f32[768,128]{1,0:T(8,128)S(1)}, u32[]{:S(2)}) copy-start(f32[768,128]{1,0:T(8,128)S(1)} %divide_subtract_fusion) | copy-start | bytes 1179652
  597.8 115.5 %all-reduce.21.cloned.1.call-start = ((), (), s32[]{:S(2)}) async-start(), calls=%async_computation.10 | async-start | bytes 2097152 | tf_op jit(solution)/shard_map/psum | solution.py:11
  661.8 154.7 %all-reduce.23.cloned.1.call-start = ((), (), s32[]{:S(2)}) async-start(), calls=%async_computation.11 | async-start | bytes 4194304 | tf_op jit(solution)/shard_map/psum | solution.py:63
  816.5 6.9 copy-start.1
Sparse Core Ops, SparseCore 0:
  13.0 50.4 reduce-scatter.1
  65.0 49.3 all-gather.2
  116.3 70.7 all-gather.4
  242.7 36.9 all-reduce.8
  303.8 61.4 all-reduce.10
  368.2 50.9 all-reduce.12
  461.7 61.0 all-reduce.14
  536.8 36.0 all-reduce.16
  597.9 61.5 all-reduce.18
  662.3 50.9 all-reduce.20
  755.5 61.0 all-reduce.22
where the time goes:
time: 834 us; the launch traced here: 830 us
  waiting for transfers between devices  592 us (71%)
  matrix products  194 us (23%)
  other arithmetic  17.6 us (2%)
  between operations  14.2 us (2%)
  local copies, waits for them, and re-layouts  12.6 us (2%)
    psum x2, waiting for transfers between devices, on_device(): gradient = lax.psum(local_grad, 'row')  123 us
    psum x2, waiting for transfers between devices, on_device(): current = current - step_size * lax.psum(product_term, 'row')  120 us
    psum x2, waiting for transfers between devices, broadcast(): return lax.psum(block, axis)  103 us
    dot_general x2, matrix products, on_device(): jnp.dot(inverse_tiles, grad_block, precision=highest, preferred_element_t...  84.5 us
    psum x2, waiting for transfers between devices, on_device(): predicted = lax.psum(local_pred, 'col')  73.2 us
    all_gather x1, waiting for transfers between devices, on_device(): land_full = lax.all_gather(landmarks, 'row', axis=1, tiled=True)  70.6 us
    reduce_scatter x1, waiting for transfers between devices, on_device(): lax.psum_scatter(jnp.dot(documents, projection, precision=highest, prefer...  50.5 us
    all_gather x1, waiting for transfers between devices, on_device(): rows_in = lax.all_gather(proj_share, 'col', axis=0, tiled=True)  50.2 us
  transfers between devices with their start and end apart: 11, of which 11 were waited for; matrix products, arithmetic and copies ran while one was open for 0% of the time, Pallas kernels for 0%

commit v1 on v0

--- a/solution.py
+++ b/solution.py
@@ -12,6 +12,19 @@
 
 
 def on_device(documents, projection, landmarks, coefficients, inverse_tiles, labels):
+
+    def link_samples(panel):
+        how_many = lax.psum(1, axis_name="col")
+        arr_next = [None] * how_many
+        arr_next[how_many - 1] = panel
+        copies = tuple(((ii, (ii + 1) % how_many) for ii in range(how_many)))
+        for it in range(how_many - 2, -1, -1):
+            arr_next[it] = lax.ppermute(arr_next[it + 1], axis_name="col", perm=copies)
+        w1 = jnp.roll(
+            jnp.concatenate(arr_next, axis=0), (lax.axis_index("col") + 1) * panel.shape[0], axis=0
+        )
+        return w1
+
     highest = lax.Precision.HIGHEST
     land_full = lax.all_gather(landmarks, "row", axis=1, tiled=True)
     sq_land = jnp.sum(land_full * land_full, axis=1)
@@ -22,7 +35,7 @@
         scatter_dimension=0,
         tiled=True,
     )
-    rows_in = lax.all_gather(proj_share, "col", axis=0, tiled=True)
+    rows_in = link_samples(proj_share)
     sq_doc = jnp.sum(rows_in * rows_in, axis=1)
     inner = lax.dot_general(
         rows_in,

time: 834 us -> 760 us (0.911)
  waiting for transfers between devices: 592 us -> 511 us
    all_gather x1, waiting for transfers between devices: 70.6 us -> 0.03 us  [on_device(): land_full = lax.all_gather(landmarks, 'row', axis=1, tiled=True)]
    all_gather x1 -> x0, waiting for transfers between devices: 50.2 us -> none  [on_device(): rows_in = lax.all_gather(proj_share, 'col', axis=0, tiled=True)]
    ppermute x0 -> x3, waiting for transfers between devices: none -> 46.2 us  [link_samples(): arr_next[it] = lax.ppermute(arr_next[it + 1], axis_name='col', perm=copies)]
  transfers between devices with their start and end apart: 11 -> 13, of which waited for: 11 -> 12; matrix products, arithmetic and copies ran while one was open for 0% -> 0% of each run, Pallas kernels for 0% -> 0%
where the time goes in v1:
time: 760 us; the launch traced here: 756 us
  waiting for transfers between devices  511 us (67%)
  matrix products  195 us (26%)
  local copies, waits for them, and re-layouts  16.1 us (2%)
  between operations  16.1 us (2%)
  other arithmetic  15.9 us (2%)
    psum x2, waiting for transfers between devices, on_device(): gradient = lax.psum(local_grad, 'row')  122 us
    psum x2, waiting for transfers between devices, on_device(): current = current - step_size * lax.psum(product_term, 'row')  119 us
    psum x2, waiting for transfers between devices, broadcast(): return lax.psum(block, axis)  103 us
    dot_general x2, matrix products, on_device(): jnp.dot(inverse_tiles, grad_block, precision=highest, preferred_element_t...  84.5 us
    psum x2, waiting for transfers between devices, on_device(): predicted = lax.psum(local_pred, 'col')  71.6 us
    reduce_scatter x1, waiting for transfers between devices, on_device(): lax.psum_scatter(jnp.dot(documents, projection, precision=highest, prefer...  49.9 us
    dot_general x2, matrix products, on_device(): lax.dot_general(kernel, residual, (((0,), (0,)), ((), ())), precision=hig...  47.6 us
    ppermute x3, waiting for transfers between devices, link_samples(): arr_next[it] = lax.ppermute(arr_next[it + 1], axis_name='col', perm=copies)  46.2 us
  transfers between devices with their start and end apart: 13, of which 12 were waited for; matrix products, arithmetic and copies ran while one was open for 0% of the time, Pallas kernels for 0%

profile of v1, /device:TPU:0, one launch (start us, length us, event | category | flops | bytes accessed | tf_op | source)
XLA Modules:
  0.0 755.9 jit_solution(9313436606771070671)
XLA Ops:
  9.1 4.6 fusion.13
  14.3 49.9 %reduce-scatter.2.cloned.1.call-done = f32[192,768]{1,0:T(8,128)} async-done(((f32[768,768]{1,0:T(8,128)}), f32[192,768]{1,0:T(8,128)}) %reduce-scatter.2.cloned.1.call-update) | async-done | bytes 589840 | tf_op jit(solution)/shard_map/reduce_scatter | solution.py:32
  65.1 15.8 %collective-permute-done = f32[192,768]{1,0:T(8,128)S(1)} collective-permute-done((f32[192,768]{1,0:T(8,128)}, f32[192,768]{1,0:T(8,128)S(1)}, u32[]{:S(2)}, u32[]{:S(2)}) %collective-permute-start) | collective-permute-done | bytes 589856 | tf_op jit(solution)/shard_map/ppermute | solution.py:22
  80.9 15.6 %collective-permute-done.1 = f32[192,768]{1,0:T(8,128)S(1)} collective-permute-done((f32[192,768]{1,0:T(8,128)S(1)}, f32[192,768]{1,0:T(8,128)S(1)}, u32[]{:S(2)}, u32[]{:S(2)}) %collective-permute-start.1) | collective-permute-done | bytes 589856 | tf_op jit(solution)/shard_map/ppermute | solution.py:22
  96.5 14.7 %collective-permute-done.2 = f32[192,768]{1,0:T(8,128)S(1)} collective-permute-done((f32[192,768]{1,0:T(8,128)S(1)}, f32[192,768]{1,0:T(8,128)S(1)}, u32[]{:S(2)}, u32[]{:S(2)}) %collective-permute-start.2) | collective-permute-done | bytes 589856 | tf_op jit(solution)/shard_map/ppermute | solution.py:22
  115.2 5.9 multiply_reduce_fusion
  123.4 34.2 %multiply_exponential_fusion = f32[768,4096]{1,0:T(8,128)S(1)} fusion(f32[4096,768]{0,1:T(8,128)S(1)} %copy-done.3, f32[4096]{0:T(1024)S(1)} %multiply_reduce_fusion, f32[768]{0:T(1024)S(1)} %multiply_reduce_fusion.1, f32[1536,768]{1,0:T(8,128)} %copy-done.6, s32[]{:T(128)S(6)} %select_n.42), kind=kOutput, calls=%fused_computation | convolution fusion | flops 29003612160 | bytes 27544580 | tf_op jit(solution)/shard_map/dot_general | solution.py:40
  157.6 4.5 copy-done.2
  162.1 10.6 %fusion.14 = f32[768,128]{1,0:T(8,128)} fusion(f32[768,4096]{1,0:T(8,128)S(1)} %multiply_exponential_fusion, f32[4096,128]{1,0:T(8,128)S(1)} %copy-done.4), kind=kOutput, calls=%fused_computation.32 | convolution fusion | flops 4831838208 | bytes 15073280 | tf_op jit(solution)/shard_map/dot_general | solution.py:60
  172.8 35.2 %all-reduce.9.cloned.1.call-done = f32[768,128]{1,0:T(8,128)} async-done(((f32[768,128]{1,0:T(8,128)}), f32[768,128]{1,0:T(8,128)}) %all-reduce.9.cloned.1.call-update) | async-done | bytes 393232 | tf_op jit(solution)/shard_map/psum | solution.py:61
  208.1 23.8 %fusion.2 = f32[4096,128]{1,0:T(8,128)} fusion(f32[768,4096]{1,0:T(8,128)} %copy-done.2, s32[768,128]{1,0:T(8,128)S(1)} %copy-done.7, f32[768,128]{1,0:T(8,128)} %all-reduce.9.cloned.1.call-done), kind=kOutput, calls=%fused_computation.12 | convolution fusion | flops 4832329728 | bytes 15466496 | tf_op jit(solution)/shard_map/dot_general | solution.py:63
  232.0 60.8 %all-reduce.11.cloned.1.call-done = f32[4096,128]{1,0:T(8,128)} async-done(((f32[4096,128]{1,0:T(8,128)}), f32[4096,128]{1,0:T(8,128)}) %all-reduce.11.cloned.1.call-update) | async-done | bytes 2097168 | tf_op jit(solution)/shard_map/psum | solution.py:70
  295.1 51.3 %all-reduce.13.cloned.1.call-done = f32[2048,128]{1,0:T(8,128)} async-done(((f32[2048,128]{1,0:T(8,128)}), f32[2048,128]{1,0:T(8,128)}) %all-reduce.13.cloned.1.call-update) | async-done | bytes 1048592 | tf_op jit(solution)/shard_map/psum | solution.py:11
  346.3 42.4 %convolution_bitcast_fusion.1 = f32[4096,128]{0,1:T(8,128)} fusion(f32[2048,128]{1,0:T(8,128)} %all-reduce.13.cloned.1.call-done, f32[4096,2048]{1,0:T(8,128)} %param.10), kind=kOutput, calls=%fused_computation.3 | convolution fusion | flops 12884901888 | bytes 36700160 | tf_op jit(solution)/shard_map/dot_general | solution.py:73
  390.8 58.4 %all-reduce.15.cloned.1.call-done = f32[4096,128]{0,1:T(8,128)} async-done(((f32[4096,128]{0,1:T(8,128)}), f32[4096,128]{0,1:T(8,128)}) %all-reduce.15.cloned.1.call-update) | async-done | bytes 2097168 | tf_op jit(solution)/shard_map/psum | solution.py:76
  449.1 13.9 %fusion.1 = f32[768,128]{1,0:T(8,128)} fusion(f32[768,4096]{1,0:T(8,128)} %copy-done.2, f32[4096,128]{0,1:T(8,128)S(1)} %copy.8, f32[4096,128]{0,1:T(8,128)} %all-reduce.15.cloned.1.call-done), kind=kOutput, calls=%fused_computation.10 | convolution fusion | flops 4832886784 | bytes 17170432 | tf_op jit(solution)/shard_map/dot_general | solution.py:60
  463.1 36.3 %all-reduce.17.cloned.1.call-done = f32[768,128]{1,0:T(8,128)} async-done(((f32[768,128]{1,0:T(8,128)}), f32[768,128]{1,0:T(8,128)}) %all-reduce.17.cloned.1.call-update) | async-done | bytes 393232 | tf_op jit(solution)/shard_map/psum | solution.py:61
  500.6 23.8 %fusion.15 = f32[4096,128]{1,0:T(8,128)} fusion(f32[768,4096]{1,0:T(8,128)} %copy-done.2, f32[768,128]{1,0:T(8,128)S(1)} %divide_subtract_fusion), kind=kOutput, calls=%fused_computation.33 | convolution fusion | flops 4831838208 | bytes 15073280 | tf_op jit(solution)/shard_map/dot_general | solution.py:63
  524.4 60.8 %all-reduce.19.cloned.1.call-done = f32[4096,128]{1,0:T(8,128)} async-done(((f32[4096,128]{1,0:T(8,128)}), f32[4096,128]{1,0:T(8,128)}) %all-reduce.19.cloned.1.call-update) | async-done | bytes 2097168 | tf_op jit(solution)/shard_map/psum | solution.py:70
  587.6 51.3 %all-reduce.21.cloned.1.call-done = f32[2048,128]{1,0:T(8,128)} async-done(((f32[2048,128]{1,0:T(8,128)}), f32[2048,128]{1,0:T(8,128)}) %all-reduce.21.cloned.1.call-update) | async-done | bytes 1048592 | tf_op jit(solution)/shard_map/psum | solution.py:11
  638.8 42.1 %convolution_bitcast_fusion = f32[4096,128]{0,1:T(8,128)} fusion(f32[2048,128]{1,0:T(8,128)} %all-reduce.21.cloned.1.call-done, f32[4096,2048]{1,0:T(8,128)} %param.10), kind=kOutput, calls=%fused_computation.2 | convolution fusion | flops 12884901888 | bytes 36700160 | tf_op jit(solution)/shard_map/dot_general | solution.py:73
  680.9 60.3 %all-reduce.23.cloned.1.call-done = f32[4096,128]{0,1:T(8,128)} async-done(((f32[4096,128]{0,1:T(8,128)}), f32[4096,128]{0,1:T(8,128)}) %all-reduce.23.cloned.1.call-update) | async-done | bytes 2097168 | tf_op jit(solution)/shard_map/psum | solution.py:76
  741.3 4.0 multiply_subtract_fusion
  745.3 2.9 copy.9
  (54 shorter events, 16.7 us)
Async XLA Ops:
  8.0 1.1 copy-start
  8.0 56.2 %reduce-scatter.2.cloned.1.call-start = ((), (), s32[]{:S(2)}) async-start(), calls=%async_computation.1 | async-start | bytes 2949120 | tf_op jit(solution)/shard_map/reduce_scatter | solution.py:32
  13.7 101.6 %all-gather.2.cloned.1.call-start = ((), (), s32[]{:S(2)}) async-start(), calls=%async_computation.2 | async-start | bytes 14155776 | tf_op jit(solution)/shard_map/all_gather | solution.py:29
  14.2 193.8 %all-reduce.9.cloned.1.call-start = ((), (), s32[]{:S(2)}) async-start(), calls=%async_computation.3 | async-start | bytes 786432 | tf_op jit(solution)/shard_map/psum | solution.py:61
  64.2 48.4 %copy-start.5 = (f32[192,768]{1,0:T(8,128)S(1)}, f32[192,768]{1,0:T(8,128)}, u32[]{:S(2)}) copy-start(f32[192,768]{1,0:T(8,128)} %reduce-scatter.2.cloned.1.call-done) | copy-start | bytes 1769476
  64.2 16.7 %collective-permute-start = (f32[192,768]{1,0:T(8,128)}, f32[192,768]{1,0:T(8,128)S(1)}, u32[]{:S(2)}, u32[]{:S(2)}) collective-permute-start(f32[192,768]{1,0:T(8,128)} %reduce-scatter.2.cloned.1.call-done), channel_id=1, source_target_pairs={{0,1},{1,2},{2,3},{3,0},{4,5},{5,6},{6,7},{7,4},{8,9},{9,10},{10,1... | collective-permute-start | bytes 1769480 | tf_op jit(solution)/shard_map/ppermute | solution.py:22
  80.9 15.6 %collective-permute-start.1 = (f32[192,768]{1,0:T(8,128)S(1)}, f32[192,768]{1,0:T(8,128)S(1)}, u32[]{:S(2)}, u32[]{:S(2)}) collective-permute-start(f32[192,768]{1,0:T(8,128)S(1)} %collective-permute-done), channel_id=1, source_target_pairs={{0,1},{1,2},{2,3},{3,0},{4,5},{5,6},{6,7},{7,4},{8,9},{9,10},{10,1... | collective-permute-start | bytes 1769480 | tf_op jit(solution)/shard_map/ppermute | solution.py:22
  96.5 14.7 %collective-permute-start.2 = (f32[192,768]{1,0:T(8,128)S(1)}, f32[192,768]{1,0:T(8,128)S(1)}, u32[]{:S(2)}, u32[]{:S(2)}) collective-permute-start(f32[192,768]{1,0:T(8,128)S(1)} %collective-permute-done.1), channel_id=1, source_target_pairs={{0,1},{1,2},{2,3},{3,0},{4,5},{5,6},{6,7},{7,4},{8,9},{9,10},{10,1... | collective-permute-start | bytes 1769480 | tf_op jit(solution)/shard_map/ppermute | solution.py:22
  112.7 2.1 copy-start.6
  115.2 8.2 %copy-start.3 = (f32[4096,768]{0,1:T(8,128)S(1)}, f32[4096,768]{0,1:T(8,128)}, u32[]{:S(2)}) copy-start(f32[4096,768]{0,1:T(8,128)} %all-gather.2.cloned.1.call-done) | copy-start | bytes 37748740
  123.4 38.8 %copy-start.4 = (f32[4096,128]{1,0:T(8,128)S(1)}, f32[4096,128]{1,0:T(8,128)}, u32[]{:S(2)}) copy-start(f32[4096,128]{1,0:T(8,128)} %param.9) | copy-start | bytes 6291460
  157.6 4.5 copy-start.2
  162.1 45.9 %copy-start.7 = (s32[768,128]{1,0:T(8,128)S(1)}, s32[768,128]{1,0:T(8,128)}, u32[]{:S(2)}) copy-start(s32[768,128]{1,0:T(8,128)} %param.11) | copy-start | bytes 1179652
  172.8 119.9 %all-reduce.11.cloned.1.call-start = ((), (), s32[]{:S(2)}) async-start(), calls=%async_computation.4 | async-start | bytes 4194304 | tf_op jit(solution)/shard_map/psum | solution.py:70
  231.9 114.4 %all-reduce.13.cloned.1.call-start = ((), (), s32[]{:S(2)}) async-start(), calls=%async_computation.5 | async-start | bytes 2097152 | tf_op jit(solution)/shard_map/psum | solution.py:11
  295.0 154.1 %all-reduce.15.cloned.1.call-start = ((), (), s32[]{:S(2)}) async-start(), calls=%async_computation.6 | async-start | bytes 4194304 | tf_op jit(solution)/shard_map/psum | solution.py:76
  388.8 110.6 %all-reduce.17.cloned.1.call-start = ((), (), s32[]{:S(2)}) async-start(), calls=%async_computation.7 | async-start | bytes 786432 | tf_op jit(solution)/shard_map/psum | solution.py:61
  463.1 122.2 %all-reduce.19.cloned.1.call-start = ((), (), s32[]{:S(2)}) async-start(), calls=%async_computation.8 | async-start | bytes 4194304 | tf_op jit(solution)/shard_map/psum | solution.py:70
  500.5 23.8 %copy-start.8 = (f32[768,128]{1,0:T(8,128)}, f32[768,128]{1,0:T(8,128)S(1)}, u32[]{:S(2)}) copy-start(f32[768,128]{1,0:T(8,128)S(1)} %divide_subtract_fusion) | copy-start | bytes 1179652
  524.4 114.4 %all-reduce.21.cloned.1.call-start = ((), (), s32[]{:S(2)}) async-start(), calls=%async_computation.9 | async-start | bytes 2097152 | tf_op jit(solution)/shard_map/psum | solution.py:11
  587.5 153.8 %all-reduce.23.cloned.1.call-start = ((), (), s32[]{:S(2)}) async-start(), calls=%async_computation.10 | async-start | bytes 4194304 | tf_op jit(solution)/shard_map/psum | solution.py:76
  680.9 67.2 %copy-start.1 = (f32[768,192]{0,1:T(8,128)S(1)}, f32[768,192]{0,1:T(8,128)}, u32[]{:S(2)}) copy-start(f32[768,192]{0,1:T(8,128)} %param.6) | copy-start | bytes 1769476
Sparse Core Ops, SparseCore 0:
  13.8 50.4 reduce-scatter.1
  172.9 35.1 all-reduce.8
  295.1 51.1 all-reduce.12
  463.2 36.2 all-reduce.16
  587.6 51.1 all-reduce.20
Sparse Core Ops, SparseCore 1:
  16.0 74.6 all-gather.1
  232.0 60.7 all-reduce.10
  388.9 60.2 all-reduce.14
  524.5 60.7 all-reduce.18
  681.0 60.2 all-reduce.22
